TPU v7x, 128 devices: a whole 4x4x4 slice. The times are simulated.
128 devices in a mesh: dp: 32 (over z, y_hi, x), tensor: 4 (over y_lo, core).
Axes of the slice: x: 4, y: 4 (y_hi: 2, y_lo: 2; y = y_hi * 2 + y_lo), z: 4, core: 2. Of those that a mesh axis runs over, the one named last changes fastest.
Arguments:
- tokens: bfloat16 [32, 4, 128, 2048], P('dp', 'tensor'), may hold values from -6 to 6
- doc_ids: int32 [32, 4, 128], P('dp'), may hold values from 0 to 3, never falling along the last dimension, each value on 1 to 64 neighbouring positions
- attn_gain: float32 [2048], P(('dp', 'tensor')), may hold values from 0.5 to 1.5
- forget_floor: float32 [2048], P(('dp', 'tensor')), may hold values from 0.5 to 0.98
- w_query: bfloat16 [2048, 2048], P('dp', 'tensor'), may hold values from -0.125 to 0.125
- w_forget: bfloat16 [2048, 2048], P('dp', 'tensor'), may hold values from -0.125 to 0.125
- w_value: bfloat16 [2048, 2048], P('dp', 'tensor'), may hold values from -0.125 to 0.125
- w_outgate: bfloat16 [2048, 2048], P('dp', 'tensor'), may hold values from -0.125 to 0.125
- w_output: bfloat16 [2048, 2048], P('tensor', 'dp'), may hold values from -0.125 to 0.125
- mlp_gain: float32 [2048], P(('dp', 'tensor')), may hold values from 0.5 to 1.5
- w_gate: bfloat16 [2048, 5632], P('dp', 'tensor'), may hold values from -0.125 to 0.125
- w_up: bfloat16 [2048, 5632], P('dp', 'tensor'), may hold values from -0.125 to 0.125
- w_down: bfloat16 [5632, 2048], P('tensor', 'dp'), may hold values from -0.078125 to 0.078125
- cotangent: bfloat16 [32, 4, 128, 2048], P('dp', 'tensor'), may hold values from -6 to 6
Outputs:
- layer_out: bfloat16 [32, 4, 128, 2048], P('dp', 'tensor')
- grad_tokens: float32 [32, 4, 128, 2048], P('dp', 'tensor')
- grad_attn_gain: float32 [2048], P(('dp', 'tensor'))
- grad_floor: float32 [2048], P(('dp', 'tensor'))
- grad_query: float32 [2048, 2048], P('dp', 'tensor')
- grad_forget: float32 [2048, 2048], P('dp', 'tensor')
- grad_value: float32 [2048, 2048], P('dp', 'tensor')
- grad_outgate: float32 [2048, 2048], P('dp', 'tensor')
- grad_output: float32 [2048, 2048], P('tensor', 'dp')
- grad_mlp_gain: float32 [2048], P(('dp', 'tensor'))
- grad_gate: float32 [2048, 5632], P('dp', 'tensor')
- grad_up: float32 [2048, 5632], P('dp', 'tensor')
- grad_down: float32 [5632, 2048], P('tensor', 'dp')
Inputs may be any that keep to these rules, and one draw needn't show every extreme that they name: `doc_ids`: within each row of 128 tokens the sequence numbers never fall; each sequence has 1 to 64 tokens, and the longest has exactly 64.
All inputs are finite; a program needn't handle non-finite values.
Results may differ from a plain program's by a relative error of at most 0.025.
Values may be sent and summed in bfloat16 or wider, within the bound.
No kernel may reach another device: no remote copies, remote signals or barrier semaphores. Data moves between devices by JAX's collectives and lax.ppermute only.
A program may use at most 192 MiB of HBM per device.

v0:
```python
import jax
import jax.numpy as jnp
from jax import lax
from jax.sharding import PartitionSpec as P

HK = 128
HIGHEST = lax.Precision.HIGHEST
epsilon = 1e-06


def row_scale(values):
    return lax.rsqrt(jnp.mean(values * values, axis=-1, keepdims=True) + epsilon)


def silu_slope(values):
    sigmoid_val = jax.nn.sigmoid(values)
    return sigmoid_val * (1.0 + values * (1.0 - sigmoid_val))


def matmul_plain(left, right):
    return jnp.dot(left, right, preferred_element_type=jnp.float32)


def times_trans(left, right):
    return lax.dot_general(
        left, right, (((1,), (1,)), ((), ())), preferred_element_type=jnp.float32
    )


def trans_times(left, right):
    return lax.dot_general(
        left, right, (((0,), (0,)), ((), ())), preferred_element_type=jnp.float32
    )


def recurrence(query, forget_raw, value, floor_vec, doc_rows):
    length = query.shape[1]
    forget = floor_vec + (1.0 - floor_vec) * jax.nn.sigmoid(forget_raw)
    log_forget = jnp.log(forget)
    keyed = 1.0 - forget
    position = jnp.arange(length)
    same_doc = doc_rows[:, :, None] == doc_rows[:, None, :]
    causal = same_doc & (position[:, None] >= position[None, :])
    starts = jnp.concatenate(
        [jnp.zeros_like(doc_rows[:, :1], dtype=bool), doc_rows[:, 1:] == doc_rows[:, :-1]], axis=1
    )
    summing = (causal & starts[:, None, :]).astype(jnp.float32)
    running = jnp.einsum("rij,rjhk->rihk", summing, log_forget, precision=HIGHEST)
    query_t = query * jnp.exp(running)
    key_t = keyed * jnp.exp(-running)
    scores = jnp.einsum("rihk,rjhk->rhij", query_t, key_t, precision=HIGHEST)
    scores = jnp.where(causal[:, None], scores, 0.0)
    return jnp.einsum("rhij,rjhv->rihv", scores, value, precision=HIGHEST)


ON_CHIP = [(0, 1), (1, 0), (2, 3), (3, 2)]
ACROSS = [(0, 2), (2, 0), (1, 3), (3, 1)]
SLOT_XOR = (0, 2, 1, 3)


def row_gather(values):
    across = lax.ppermute(values, "tensor", ACROSS)
    pair = jnp.stack([values, across])
    other = lax.ppermute(pair, "tensor", ON_CHIP)
    return jnp.concatenate([pair, other]).reshape((-1,) + values.shape[1:])


def row_sum(values):
    blocks = values.reshape((4, -1) + values.shape[1:])
    got = lax.ppermute(blocks[2:], "tensor", ON_CHIP)
    mine = blocks[0] + got[0]
    theirs = blocks[1] + got[1]
    return mine + lax.ppermute(theirs, "tensor", ACROSS)


def spread_sum(values, axis, count):
    blocks = values.reshape((count, -1) + values.shape[1:])
    got = lax.all_to_all(blocks, axis, 0, 0, tiled=False)
    return got.astype(jnp.float32).sum(axis=0)


def small_gather(vectors):
    count = 128
    spread = jnp.broadcast_to(vectors[None], (count,) + vectors.shape)
    got = lax.all_to_all(spread, ("dp", "tensor"), 0, 0, tiled=False)
    return jnp.swapaxes(got, 0, 1).reshape(vectors.shape[0], -1)


def small_sum(vectors):
    count = 128
    blocks = vectors.reshape(vectors.shape[0], count, -1)
    got = lax.all_to_all(jnp.swapaxes(blocks, 0, 1), ("dp", "tensor"), 0, 0, tiled=False)
    return got.sum(axis=0)


def shards(
    tokens,
    doc_ids,
    attn_gain,
    forget_floor,
    w_query,
    w_forget,
    w_value,
    w_outgate,
    w_output,
    mlp_gain,
    w_gate,
    w_up,
    w_down,
    cotangent,
):
    gains = small_gather(jnp.stack([attn_gain, forget_floor, mlp_gain]))
    attn_full, floor_full, mlp_full = (gains[0], gains[1], gains[2])
    part_index = lax.axis_index("tensor")
    local_width = w_query.shape[1]
    local_heads = local_width // HK
    hidden_width = w_gate.shape[1]
    floor_local = lax.dynamic_slice_in_dim(
        floor_full, part_index * local_width, local_width
    ).reshape(local_heads, HK)
    model_width = attn_full.shape[0]
    slot_rows = jnp.bitwise_xor(part_index, jnp.array(SLOT_XOR, jnp.int32))
    doc_all = jnp.take(doc_ids[0], slot_rows, axis=0)
    row_count = doc_all.shape[0]
    resid_in = tokens[0].reshape(-1, model_width).astype(jnp.float32)
    cot_local = cotangent[0].reshape(-1, model_width)
    attn_pack = jnp.concatenate([w_query, w_forget, w_value, w_outgate, w_output.T], axis=1)
    mlp_pack = jnp.concatenate([w_gate, w_up, w_down.T], axis=1)
    attn_all = lax.all_gather(attn_pack, "dp", axis=0, tiled=True)
    mlp_all = lax.all_gather(mlp_pack, "dp", axis=0, tiled=True)
    wq_all = attn_all[:, 0 * local_width : 1 * local_width]
    wf_all = attn_all[:, 1 * local_width : 2 * local_width]
    wv_all = attn_all[:, 2 * local_width : 3 * local_width]
    wg_all = attn_all[:, 3 * local_width : 4 * local_width]
    wo_t = attn_all[:, 4 * local_width : 5 * local_width]
    wgate_all = mlp_all[:, 0:hidden_width]
    wup_all = mlp_all[:, hidden_width : 2 * hidden_width]
    wdown_t = mlp_all[:, 2 * hidden_width : 3 * hidden_width]
    scale_one = row_scale(resid_in)
    normed = row_gather((resid_in * scale_one * attn_full).astype(jnp.bfloat16))
    query = matmul_plain(normed, wq_all)
    forget_raw = matmul_plain(normed, wf_all)
    value = matmul_plain(normed, wv_all)
    out_gate = matmul_plain(normed, wg_all)

    def mixer(query_in, forget_in, value_in, floor_in):

        def shaped(arr):
            return arr.reshape(row_count, -1, local_heads, HK)

        mixed_rows = recurrence(
            shaped(query_in), shaped(forget_in), shaped(value_in), floor_in, doc_all
        )
        return mixed_rows.reshape(query_in.shape[0], local_width)

    mixed, pullback = jax.vjp(mixer, query, forget_raw, value, floor_local)
    gate_act = jax.nn.silu(out_gate)
    gated = (mixed * gate_act).astype(jnp.bfloat16)
    branch = row_sum(times_trans(gated, wo_t))
    resid = resid_in + branch
    scale_two = row_scale(resid)
    normed2 = row_gather((resid * scale_two * mlp_full).astype(jnp.bfloat16))
    gate_proj = matmul_plain(normed2, wgate_all)
    up_proj = matmul_plain(normed2, wup_all)
    gate_silu = jax.nn.silu(gate_proj)
    hidden = (gate_silu * up_proj).astype(jnp.bfloat16)
    ffn_out = row_sum(times_trans(hidden, wdown_t))
    layer_out = (resid + ffn_out).astype(jnp.bfloat16).reshape(tokens.shape)
    cot_full = row_gather(cot_local)
    d_hidden = matmul_plain(cot_full, wdown_t)
    grad_down_t = trans_times(cot_full, hidden)
    d_gate = (d_hidden * up_proj * silu_slope(gate_proj)).astype(jnp.bfloat16)
    d_up = (d_hidden * gate_silu).astype(jnp.bfloat16)
    grad_gate = trans_times(normed2, d_gate)
    grad_up = trans_times(normed2, d_up)
    mlp_grads = jnp.concatenate(
        [
            grad_gate.astype(jnp.bfloat16),
            grad_up.astype(jnp.bfloat16),
            grad_down_t.astype(jnp.bfloat16),
        ],
        axis=1,
    )
    mlp_red = lax.psum_scatter(mlp_grads, "dp", scatter_dimension=0, tiled=True).astype(jnp.float32)
    d_normed2 = row_sum(times_trans(d_gate, wgate_all) + times_trans(d_up, wup_all))
    grad_mlp = jnp.sum(d_normed2 * resid * scale_two, axis=0)
    inner_two = jnp.mean(d_normed2 * mlp_full * resid, axis=-1, keepdims=True)
    d_resid = (
        cot_local.astype(jnp.float32)
        + d_normed2 * mlp_full * scale_two
        - resid * scale_two**3 * inner_two
    )
    d_branch = row_gather(d_resid.astype(jnp.bfloat16))
    d_gated = matmul_plain(d_branch, wo_t)
    grad_output_t = trans_times(d_branch, gated)
    d_mixed = d_gated * gate_act
    d_outgate = (d_gated * mixed * silu_slope(out_gate)).astype(jnp.bfloat16)
    d_query, d_forget, d_value, d_floor = pullback(d_mixed)
    d_query = d_query.astype(jnp.bfloat16)
    d_forget = d_forget.astype(jnp.bfloat16)
    d_value = d_value.astype(jnp.bfloat16)
    grad_query = trans_times(normed, d_query)
    grad_forget = trans_times(normed, d_forget)
    grad_value = trans_times(normed, d_value)
    grad_outgate = trans_times(normed, d_outgate)
    attn_grads = jnp.concatenate(
        [
            grad_query.astype(jnp.bfloat16),
            grad_forget.astype(jnp.bfloat16),
            grad_value.astype(jnp.bfloat16),
            grad_outgate.astype(jnp.bfloat16),
            grad_output_t.astype(jnp.bfloat16),
        ],
        axis=1,
    )
    attn_red = spread_sum(attn_grads, "dp", 32)
    d_normed = row_sum(
        times_trans(d_query, wq_all)
        + times_trans(d_forget, wf_all)
        + times_trans(d_value, wv_all)
        + times_trans(d_outgate, wg_all)
    )
    grad_attn = jnp.sum(d_normed * resid_in * scale_one, axis=0)
    inner_one = jnp.mean(d_normed * attn_full * resid_in, axis=-1, keepdims=True)
    grad_tokens = (
        d_resid + d_normed * attn_full * scale_one - resid_in * scale_one**3 * inner_one
    ).reshape(tokens.shape)
    floor_vector = lax.dynamic_update_slice(
        jnp.zeros((model_width,), jnp.float32), d_floor.reshape(-1), (part_index * local_width,)
    )
    reduced_small = small_sum(jnp.stack([grad_attn, floor_vector, grad_mlp]))
    return (
        layer_out,
        grad_tokens,
        reduced_small[0],
        reduced_small[1],
        attn_red[:, 0 * local_width : 1 * local_width],
        attn_red[:, 1 * local_width : 2 * local_width],
        attn_red[:, 2 * local_width : 3 * local_width],
        attn_red[:, 3 * local_width : 4 * local_width],
        attn_red[:, 4 * local_width : 5 * local_width].T,
        reduced_small[2],
        mlp_red[:, 0:hidden_width],
        mlp_red[:, hidden_width : 2 * hidden_width],
        mlp_red[:, 2 * hidden_width : 3 * hidden_width].T,
    )


def solution(mesh):
    return jax.shard_map(
        shards,
        mesh=mesh,
        in_specs=(
            P("dp", "tensor", None, None),
            P("dp", None, None),
            P(("dp", "tensor")),
            P(("dp", "tensor")),
            P("dp", "tensor"),
            P("dp", "tensor"),
            P("dp", "tensor"),
            P("dp", "tensor"),
            P("tensor", "dp"),
            P(("dp", "tensor")),
            P("dp", "tensor"),
            P("dp", "tensor"),
            P("tensor", "dp"),
            P("dp", "tensor", None, None),
        ),
        out_specs=(
            P("dp", "tensor", None, None),
            P("dp", "tensor", None, None),
            P(("dp", "tensor")),
            P(("dp", "tensor")),
            P("dp", "tensor"),
            P("dp", "tensor"),
            P("dp", "tensor"),
            P("dp", "tensor"),
            P("tensor", "dp"),
            P(("dp", "tensor")),
            P("dp", "tensor"),
            P("dp", "tensor"),
            P("tensor", "dp"),
        ),
        check_vma=False,
    )
```

profile of v0, /device:TPU:0, one launch (start us, length us, event | category | flops | bytes accessed | tf_op | source)
XLA Modules:
  0.0 807.6 jit_solution(461497468060412222)
XLA Ops:
  15.1 11.1 %all-to-all-start = ((f32[128,3,16]{2,1,0:T(4,128)}), f32[128,3,16]{2,1,0:T(4,128)S(1)}, u32[]{:S(2)}, u32[]{:S(2)}) async-start(f32[128,3,16]{2,1,0:T(4,128)} %broadcast_in_dim.29), calls=%async_computation | async-start | bytes 524288 | tf_op jit(solution)/shard_map/all_to_all | solution.py:85
  27.1 11.5 %all-to-all-done = f32[128,3,16]{2,1,0:T(4,128)S(1)} async-done(((f32[128,3,16]{2,1,0:T(4,128)}), f32[128,3,16]{2,1,0:T(4,128)S(1)}, u32[]{:S(2)}, u32[]{:S(2)}) %all-to-all-start) | async-done | bytes 24608 | tf_op jit(solution)/shard_map/all_to_all | solution.py:85
  40.2 15.4 %collective-permute-done = bf16[128,2048]{1,0:T(8,128)(2,1)S(1)} collective-permute-done((bf16[128,2048]{1,0:T(8,128)(2,1)S(1)}, bf16[128,2048]{1,0:T(8,128)(2,1)S(1)}, u32[]{:S(2)}, u32[]{:S(2)}) %collective-permute-start) | collective-permute-done | bytes 524320 | tf_op jit(solution)/shard_map/ppermute | solution.py:62
  61.4 72.5 %all-gather.3.cloned.1.call-done = bf16[2048,2560]{1,0:T(8,128)(2,1)} async-done(((bf16[64,2560]{1,0:T(8,128)(2,1)}), bf16[2048,2560]{1,0:T(8,128)(2,1)}) %all-gather.3.cloned.1.call-update) | async-done | bytes 10485776 | tf_op jit(solution)/shard_map/all_gather | solution.py:129
  182.8 26.3 %collective-permute-done.3 = f32[128,2048]{1,0:T(8,128)} collective-permute-done((f32[128,2048]{1,0:T(8,128)S(1)}, f32[128,2048]{1,0:T(8,128)}, u32[]{:S(2)}, u32[]{:S(2)}) %collective-permute-start.3) | collective-permute-done | bytes 1048608 | tf_op jit(solution)/shard_map/ppermute | solution.py:73
  211.9 13.1 %collective-permute-done.8 = bf16[128,2048]{1,0:T(8,128)(2,1)} collective-permute-done((bf16[128,2048]{1,0:T(8,128)(2,1)S(1)}, bf16[128,2048]{1,0:T(8,128)(2,1)}, u32[]{:S(2)}, u32[]{:S(2)}) %collective-permute-start.8) | collective-permute-done | bytes 524320 | tf_op jit(solution)/shard_map/ppermute | solution.py:62
  226.3 20.7 %collective-permute-done.4 = bf16[128,2048]{1,0:T(8,128)(2,1)S(1)} collective-permute-done((bf16[128,2048]{1,0:T(8,128)(2,1)S(1)}, bf16[128,2048]{1,0:T(8,128)(2,1)S(1)}, u32[]{:S(2)}, u32[]{:S(2)}) %collective-permute-start.4) | collective-permute-done | bytes 524320 | tf_op jit(solution)/shard_map/ppermute | solution.py:62
  251.4 63.5 %all-gather.5.cloned.1.call-done = bf16[2048,4224]{1,0:T(8,128)(2,1)} async-done(((bf16[64,4224]{1,0:T(8,128)(2,1)}), bf16[2048,4224]{1,0:T(8,128)(2,1)}) %all-gather.5.cloned.1.call-update) | async-done | bytes 17301520 | tf_op jit(solution)/shard_map/all_gather | solution.py:130
  315.0 7.0 fusion
  327.3 7.3 multiply_convert_fusion.1
  345.1 7.9 pad_maximum_fusion
  353.0 21.9 %copy.106 = bf16[2048,4224]{1,0:T(8,128)(2,1)} copy(bf16[2048,4224]{0,1:T(8,128)(2,1)} %pad_maximum_fusion) | data formatting | bytes 34603008
  374.9 6.0 fusion.4
  381.0 5.6 fusion.12
  398.6 29.0 %collective-permute-done.11 = f32[128,2048]{1,0:T(8,128)S(1)} collective-permute-done((f32[128,2048]{1,0:T(8,128)S(1)}, f32[128,2048]{1,0:T(8,128)S(1)}, u32[]{:S(2)}, u32[]{:S(2)}) %collective-permute-start.11) | collective-permute-done | bytes 1048608 | tf_op jit(solution)/shard_map/ppermute | solution.py:73
  428.1 29.3 %collective-permute-done.7 = f32[128,2048]{1,0:T(8,128)S(1)} collective-permute-done((f32[128,2048]{1,0:T(8,128)S(1)}, f32[128,2048]{1,0:T(8,128)S(1)}, u32[]{:S(2)}, u32[]{:S(2)}) %collective-permute-start.7) | collective-permute-done | bytes 1048608 | tf_op jit(solution)/shard_map/ppermute | solution.py:73
  459.6 17.0 %collective-permute-done.12 = bf16[128,2048]{1,0:T(8,128)(2,1)S(1)} collective-permute-done((bf16[128,2048]{1,0:T(8,128)(2,1)S(1)}, bf16[128,2048]{1,0:T(8,128)(2,1)S(1)}, u32[]{:S(2)}, u32[]{:S(2)}) %collective-permute-start.12) | collective-permute-done | bytes 524320 | tf_op jit(solution)/shard_map/ppermute | solution.py:62
  528.4 21.0 %collective-permute-done.15 = f32[128,2048]{1,0:T(8,128)} collective-permute-done((f32[128,2048]{1,0:T(8,128)S(1)}, f32[128,2048]{1,0:T(8,128)}, u32[]{:S(2)}, u32[]{:S(2)}) %collective-permute-start.15) | collective-permute-done | bytes 1048608 | tf_op jit(solution)/shard_map/ppermute | solution.py:73
  552.6 7.2 all-to-all-start.1
  564.0 13.9 %copy.92 = bf16[2048,2560]{1,0:T(8,128)(2,1)} copy(bf16[2048,2560]{0,1:T(8,128)(2,1)} %fusion.15) | data formatting | bytes 20971520 | tf_op jit(solution)/shard_map/concatenate | solution.py:206
  578.0 9.8 %all-to-all-start.2 = ((bf16[32,64,2560]{2,1,0:T(8,128)(2,1)}), bf16[32,64,2560]{2,1,0:T(8,128)(2,1)}, u32[]{:S(2)}, u32[]{:S(2)}) async-start(bf16[32,64,2560]{2,1,0:T(8,128)(2,1)} %bitcast.265), calls=%async_computation.2 | async-start | bytes 20971520 | tf_op jit(solution)/shard_map/all_to_all | solution.py:78
  589.7 163.9 %all-to-all-done.2 = bf16[32,64,2560]{2,1,0:T(8,128)(2,1)} async-done(((bf16[32,64,2560]{2,1,0:T(8,128)(2,1)}), bf16[32,64,2560]{2,1,0:T(8,128)(2,1)}, u32[]{:S(2)}, u32[]{:S(2)}) %all-to-all-start.2) | async-done | bytes 10485792 | tf_op jit(solution)/shard_map/all_to_all | solution.py:78
  753.7 5.8 convert_reduce_fusion
  760.3 31.9 %reduce-scatter.4.cloned.1.call-done = bf16[64,4224]{1,0:T(8,128)(2,1)} async-done(((bf16[2048,4224]{1,0:T(8,128)(2,1)}), bf16[64,4224]{1,0:T(8,128)(2,1)}) %reduce-scatter.4.cloned.1.call-update) | async-done | bytes 540688
  (234 shorter events, 173.8 us)
Async XLA Ops:
  7.2 48.7 %copy-start = (s32[1,4,128]{2,1,0:T(4,128)S(1)}, s32[1,4,128]{2,1,0:T(4,128)}, u32[]{:S(2)}) copy-start(s32[1,4,128]{2,1,0:T(4,128)} %param.16) | copy-start | bytes 6148
  7.2 126.6 %all-gather.3.cloned.1.call-start = ((), (), s32[]{:S(2)}) async-start(), calls=%async_computation.4 | async-start | bytes 10813440 | tf_op jit(solution)/shard_map/all_gather | solution.py:129
  12.3 302.7 %all-gather.5.cloned.1.call-start = ((), (), s32[]{:S(2)}) async-start(), calls=%async_computation.5 | async-start | bytes 17842176 | tf_op jit(solution)/shard_map/all_gather | solution.py:130
  15.1 23.4 %all-to-all-start = ((f32[128,3,16]{2,1,0:T(4,128)}), f32[128,3,16]{2,1,0:T(4,128)S(1)}, u32[]{:S(2)}, u32[]{:S(2)}) async-start(f32[128,3,16]{2,1,0:T(4,128)} %broadcast_in_dim.29), calls=%async_computation | async-start | bytes 524288 | tf_op jit(solution)/shard_map/all_to_all | solution.py:85
  26.3 765.9 %reduce-scatter.4.cloned.1.call-start = ((), (), s32[]{:S(2)}) async-start(), calls=%async_computation.6 | async-start | bytes 17842176
  39.4 16.3 %collective-permute-start = (bf16[128,2048]{1,0:T(8,128)(2,1)S(1)}, bf16[128,2048]{1,0:T(8,128)(2,1)S(1)}, u32[]{:S(2)}, u32[]{:S(2)}) collective-permute-start(bf16[128,2048]{1,0:T(8,128)(2,1)S(1)} %fusion.62), channel_id=1, source_target_pairs={{0,2},{2,0},{1,3},{3,1},{4,6},{6,4},{5,7},{7,5},{8,10},{10,8},{9,1... | collective-permute-start | bytes 1572872 | tf_op jit(solution)/shard_map/ppermute | solution.py:62
  55.8 2.9 collective-permute-start.1
  176.3 4.2 collective-permute-start.2
  180.7 28.5 %collective-permute-start.3 = (f32[128,2048]{1,0:T(8,128)S(1)}, f32[128,2048]{1,0:T(8,128)}, u32[]{:S(2)}, u32[]{:S(2)}) collective-permute-start(f32[128,2048]{1,0:T(8,128)S(1)} %fusion.88), channel_id=1, source_target_pairs={{0,2},{2,0},{1,3},{3,1},{4,6},{6,4},{5,7},{7,5},{8,10},{10,8},{9,1... | collective-permute-start | bytes 3145736 | tf_op jit(solution)/shard_map/ppermute | solution.py:73
  181.9 43.1 %collective-permute-start.8 = (bf16[128,2048]{1,0:T(8,128)(2,1)S(1)}, bf16[128,2048]{1,0:T(8,128)(2,1)}, u32[]{:S(2)}, u32[]{:S(2)}) collective-permute-start(bf16[128,2048]{1,0:T(8,128)(2,1)S(1)} %bitcast.268), channel_id=1, source_target_pairs={{0,2},{2,0},{1,3},{3,1},{4,6},{6,4},{5,7},{7,5},{8,10},{10,8},{9,1... | collective-permute-start | bytes 1572872 | tf_op jit(solution)/shard_map/ppermute | solution.py:62
  211.6 35.5 %collective-permute-start.4 = (bf16[128,2048]{1,0:T(8,128)(2,1)S(1)}, bf16[128,2048]{1,0:T(8,128)(2,1)S(1)}, u32[]{:S(2)}, u32[]{:S(2)}) collective-permute-start(bf16[128,2048]{1,0:T(8,128)(2,1)S(1)} %multiply_convert_fusion.4), channel_id=1, source_target_pairs={{0,2},{2,0},{1,3},{3,1},{4,6},{6,4},{5,7},{7,5},{8,10},{10,8},{9,1... | collective-permute-start | bytes 1572872 | tf_op jit(solution)/shard_map/ppermute | solution.py:62
  226.1 21.1 %collective-permute-start.9 = (bf16[2,128,2048]{2,1,0:T(8,128)(2,1)S(1)}, bf16[2,128,2048]{2,1,0:T(8,128)(2,1)S(1)}, u32[]{:S(2)}, u32[]{:S(2)}) collective-permute-start(bf16[2,128,2048]{2,1,0:T(8,128)(2,1)S(1)} %pad_maximum_fusion.7), channel_id=1, source_target_pairs={{0,1},{1,0},{2,3},{3,2},{4,5},{5,4},{6,7},{7,6},{8,9},{9,8},{10,11... | collective-permute-start | bytes 3145736 | tf_op jit(solution)/shard_map/ppermute | solution.py:64
  247.1 2.7 collective-permute-start.5
  386.8 6.9 collective-permute-start.10
  393.6 4.2 collective-permute-start.6
  393.8 33.8 %collective-permute-start.11 = (f32[128,2048]{1,0:T(8,128)S(1)}, f32[128,2048]{1,0:T(8,128)S(1)}, u32[]{:S(2)}, u32[]{:S(2)}) collective-permute-start(f32[128,2048]{1,0:T(8,128)S(1)} %fusion.80), channel_id=1, source_target_pairs={{0,2},{2,0},{1,3},{3,1},{4,6},{6,4},{5,7},{7,5},{8,10},{10,8},{9,1... | collective-permute-start | bytes 3145736 | tf_op jit(solution)/shard_map/ppermute | solution.py:73
  398.0 59.4 %collective-permute-start.7 = (f32[128,2048]{1,0:T(8,128)S(1)}, f32[128,2048]{1,0:T(8,128)S(1)}, u32[]{:S(2)}, u32[]{:S(2)}) collective-permute-start(f32[128,2048]{1,0:T(8,128)S(1)} %fusion.83), channel_id=1, source_target_pairs={{0,2},{2,0},{1,3},{3,1},{4,6},{6,4},{5,7},{7,5},{8,10},{10,8},{9,1... | collective-permute-start | bytes 3145736 | tf_op jit(solution)/shard_map/ppermute | solution.py:73
  459.1 17.6 %collective-permute-start.12 = (bf16[128,2048]{1,0:T(8,128)(2,1)S(1)}, bf16[128,2048]{1,0:T(8,128)(2,1)S(1)}, u32[]{:S(2)}, u32[]{:S(2)}) collective-permute-start(bf16[128,2048]{1,0:T(8,128)(2,1)S(1)} %get-tuple-element.75), channel_id=1, source_target_pairs={{0,2},{2,0},{1,3},{3,1},{4,6},{6,4},{5,7},{7,5},{8,10},{10,8},{9,1... | collective-permute-start | bytes 1572872 | tf_op jit(solution)/shard_map/ppermute | solution.py:62
  476.8 3.0 collective-permute-start.13
  509.9 4.5 collective-permute-start.14
  516.1 33.3 %collective-permute-start.15 = (f32[128,2048]{1,0:T(8,128)S(1)}, f32[128,2048]{1,0:T(8,128)}, u32[]{:S(2)}, u32[]{:S(2)}) collective-permute-start(f32[128,2048]{1,0:T(8,128)S(1)} %fusion.77), channel_id=1, source_target_pairs={{0,2},{2,0},{1,3},{3,1},{4,6},{6,4},{5,7},{7,5},{8,10},{10,8},{9,1... | collective-permute-start | bytes 3145736 | tf_op jit(solution)/shard_map/ppermute | solution.py:73
  528.4 31.4 %copy-start.23 = (bf16[512,512]{1,0:T(8,128)(2,1)S(1)}, bf16[512,512]{1,0:T(8,128)(2,1)}, u32[]{:S(2)}) copy-start(bf16[512,512]{1,0:T(8,128)(2,1)} %copy-done.22) | copy-start | bytes 1572868
  552.6 25.4 %all-to-all-start.1 = ((f32[128,3,16]{2,1,0:T(4,128)}), f32[128,3,16]{2,1,0:T(4,128)S(1)}, u32[]{:S(2)}, u32[]{:S(2)}) async-start(f32[128,3,16]{2,1,0:T(4,128)} %copy.91), calls=%async_computation.1 | async-start | bytes 524288 | tf_op jit(solution)/shard_map/all_to_all | solution.py:92
  578.0 175.7 %all-to-all-start.2 = ((bf16[32,64,2560]{2,1,0:T(8,128)(2,1)}), bf16[32,64,2560]{2,1,0:T(8,128)(2,1)}, u32[]{:S(2)}, u32[]{:S(2)}) async-start(bf16[32,64,2560]{2,1,0:T(8,128)(2,1)} %bitcast.265), calls=%async_computation.2 | async-start | bytes 20971520 | tf_op jit(solution)/shard_map/all_to_all | solution.py:78
  (44 other events, 298.9 us)
Sparse Core Ops, SparseCore 0:
  12.4 121.4 all-gather.2
  136.9 177.9 all-gather.4
  375.0 417.0 reduce-scatter.3
where the time goes:
time: 813 us; the launch traced here: 808 us
  waiting for transfers between devices  527 us (65%)
  matrix products  108 us (13%)
  local copies, waits for them, and re-layouts  86.1 us (11%)
  other arithmetic  37 us (5%)
  starting transfers between devices  34 us (4%)
  between operations  15.3 us (2%)
    all_to_all x1, waiting for transfers between devices, spread_sum(): got = lax.all_to_all(blocks, axis, 0, 0, tiled=False)  164 us
    ppermute x4, waiting for transfers between devices, row_sum(): return mine + lax.ppermute(theirs, 'tensor', ACROSS)  106 us
    all_gather x1, waiting for transfers between devices, shards(): attn_all = lax.all_gather(attn_pack, 'dp', axis=0, tiled=True)  72.5 us
    ppermute x4, waiting for transfers between devices, row_gather(): across = lax.ppermute(values, 'tensor', ACROSS)  66.2 us
    all_gather x1, waiting for transfers between devices, shards(): mlp_all = lax.all_gather(mlp_pack, 'dp', axis=0, tiled=True)  63.5 us
    unnamed x101, local copies, waits for them, and re-layouts  40.4 us
    dot_general x8, matrix products, matmul_plain(): return jnp.dot(left, right, preferred_element_type=jnp.float32)  36.9 us
    unnamed x4, waiting for transfers between devices  31.9 us
  transfers between devices with their start and end apart: 22, of which 19 were waited for; matrix products, arithmetic and copies ran while one was open for 19% of the time, Pallas kernels for 0%

commit v1 on v0

--- a/solution.py
+++ b/solution.py
@@ -126,8 +126,11 @@
     cot_local = cotangent[0].reshape(-1, model_width)
     attn_pack = jnp.concatenate([w_query, w_forget, w_value, w_outgate, w_output.T], axis=1)
     mlp_pack = jnp.concatenate([w_gate, w_up, w_down.T], axis=1)
-    attn_all = lax.all_gather(attn_pack, "dp", axis=0, tiled=True)
-    mlp_all = lax.all_gather(mlp_pack, "dp", axis=0, tiled=True)
+    attn_all, mlp_all = jnp.split(
+        lax.all_gather(jnp.concatenate([attn_pack, mlp_pack], axis=1), "dp", axis=0, tiled=True),
+        [attn_pack.shape[1]],
+        axis=1,
+    )
     wq_all = attn_all[:, 0 * local_width : 1 * local_width]
     wf_all = attn_all[:, 1 * local_width : 2 * local_width]
     wv_all = attn_all[:, 2 * local_width : 3 * local_width]

time: 813 us -> 844 us (1.038)
  waiting for transfers between devices: 527 us -> 555 us
    all_gather x2 -> x1, waiting for transfers between devices: 136 us -> 184 us  [shards(): lax.all_gather(jnp.concatenate([attn_pack, mlp_pack], axis=1), 'dp', axis...]
    ppermute x4, waiting for transfers between devices: 106 us -> 80.8 us  [row_sum(): return mine + lax.ppermute(theirs, 'tensor', ACROSS)]
    ppermute x4, waiting for transfers between devices: 66.2 us -> 78 us  [row_gather(): across = lax.ppermute(values, 'tensor', ACROSS)]
    all_to_all x1, waiting for transfers between devices: 164 us -> 153 us  [spread_sum(): got = lax.all_to_all(blocks, axis, 0, 0, tiled=False)]
    unnamed x4 -> x3, waiting for transfers between devices: 31.9 us -> 37.6 us
    unnamed x101 -> x98, local copies, waits for them, and re-layouts: 40.4 us -> 36.2 us
  transfers between devices with their start and end apart: 22 -> 21, of which waited for: 19 -> 16; matrix products, arithmetic and copies ran while one was open for 19% -> 14% of each run, Pallas kernels for 0% -> 0%
where the time goes in v1:
time: 844 us; the launch traced here: 839 us
  waiting for transfers between devices  555 us (66%)
  matrix products  116 us (14%)
  local copies, waits for them, and re-layouts  83.1 us (10%)
  starting transfers between devices  36.4 us (4%)
  other arithmetic  32.5 us (4%)
  between operations  15.5 us (2%)
    all_gather x1, waiting for transfers between devices, shards(): lax.all_gather(jnp.concatenate([attn_pack, mlp_pack], axis=1), 'dp', axis...  184 us
    all_to_all x1, waiting for transfers between devices, spread_sum(): got = lax.all_to_all(blocks, axis, 0, 0, tiled=False)  153 us
    ppermute x4, waiting for transfers between devices, row_sum(): return mine + lax.ppermute(theirs, 'tensor', ACROSS)  80.8 us
    ppermute x4, waiting for transfers between devices, row_gather(): across = lax.ppermute(values, 'tensor', ACROSS)  78 us
    unnamed x3, waiting for transfers between devices  37.6 us
    dot_general x8, matrix products, matmul_plain(): return jnp.dot(left, right, preferred_element_type=jnp.float32)  37.3 us
    unnamed x98, local copies, waits for them, and re-layouts  36.2 us
    dot_general x8, matrix products, times_trans(): lax.dot_general(left, right, (((1,), (1,)), ((), ())), preferred_element_...  32 us
  transfers between devices with their start and end apart: 21, of which 16 were waited for; matrix products, arithmetic and copies ran while one was open for 14% of the time, Pallas kernels for 0%

profile of v1, /device:TPU:0, one launch (start us, length us, event | category | flops | bytes accessed | tf_op | source)
XLA Modules:
  0.0 838.7 jit_solution(9228379636467242084)
XLA Ops:
  16.1 11.1 %all-to-all-start = ((f32[128,3,16]{2,1,0:T(4,128)}), f32[128,3,16]{2,1,0:T(4,128)S(1)}, u32[]{:S(2)}, u32[]{:S(2)}) async-start(f32[128,3,16]{2,1,0:T(4,128)} %broadcast_in_dim.29), calls=%async_computation | async-start | bytes 524288 | tf_op jit(solution)/shard_map/all_to_all | solution.py:85
  28.0 10.1 %all-to-all-done = f32[128,3,16]{2,1,0:T(4,128)S(1)} async-done(((f32[128,3,16]{2,1,0:T(4,128)}), f32[128,3,16]{2,1,0:T(4,128)S(1)}, u32[]{:S(2)}, u32[]{:S(2)}) %all-to-all-start) | async-done | bytes 24608 | tf_op jit(solution)/shard_map/all_to_all | solution.py:85
  39.9 13.3 %collective-permute-done = bf16[128,2048]{1,0:T(8,128)(2,1)S(1)} collective-permute-done((bf16[128,2048]{1,0:T(8,128)(2,1)S(1)}, bf16[128,2048]{1,0:T(8,128)(2,1)S(1)}, u32[]{:S(2)}, u32[]{:S(2)}) %collective-permute-start) | collective-permute-done | bytes 524320 | tf_op jit(solution)/shard_map/ppermute | solution.py:62
  59.0 184.0 %all-gather.2.cloned.1.call-done = bf16[2048,6784]{1,0:T(8,128)(2,1)} async-done(((bf16[64,6784]{1,0:T(8,128)(2,1)}), bf16[2048,6784]{1,0:T(8,128)(2,1)}) %all-gather.2.cloned.1.call-update) | async-done | bytes 27787280 | tf_op jit(solution)/shard_map/all_gather | solution.py:130
  293.2 34.5 %collective-permute-done.8 = bf16[128,2048]{1,0:T(8,128)(2,1)S(1)} collective-permute-done((bf16[128,2048]{1,0:T(8,128)(2,1)S(1)}, bf16[128,2048]{1,0:T(8,128)(2,1)S(1)}, u32[]{:S(2)}, u32[]{:S(2)}) %collective-permute-start.8) | collective-permute-done | bytes 524320 | tf_op jit(solution)/shard_map/ppermute | solution.py:62
  331.4 13.0 %collective-permute-done.4 = bf16[128,2048]{1,0:T(8,128)(2,1)S(1)} collective-permute-done((bf16[128,2048]{1,0:T(8,128)(2,1)S(1)}, bf16[128,2048]{1,0:T(8,128)(2,1)S(1)}, u32[]{:S(2)}, u32[]{:S(2)}) %collective-permute-start.4) | collective-permute-done | bytes 524320 | tf_op jit(solution)/shard_map/ppermute | solution.py:62
  344.8 5.8 fusion
  350.8 5.8 fusion.6
  356.6 7.2 multiply_convert_fusion.1
  374.2 7.9 pad_maximum_fusion
  382.1 21.3 %copy.106 = bf16[2048,4224]{1,0:T(8,128)(2,1)} copy(bf16[2048,4224]{0,1:T(8,128)(2,1)} %pad_maximum_fusion) | data formatting | bytes 34603008
  403.4 6.0 fusion.4
  409.4 5.5 fusion.12
  416.4 5.5 fusion.2
  427.2 29.4 %collective-permute-done.11 = f32[128,2048]{1,0:T(8,128)S(1)} collective-permute-done((f32[128,2048]{1,0:T(8,128)S(1)}, f32[128,2048]{1,0:T(8,128)S(1)}, u32[]{:S(2)}, u32[]{:S(2)}) %collective-permute-start.11) | collective-permute-done | bytes 1048608 | tf_op jit(solution)/shard_map/ppermute | solution.py:73
  457.1 29.1 %collective-permute-done.7 = f32[128,2048]{1,0:T(8,128)S(1)} collective-permute-done((f32[128,2048]{1,0:T(8,128)S(1)}, f32[128,2048]{1,0:T(8,128)S(1)}, u32[]{:S(2)}, u32[]{:S(2)}) %collective-permute-start.7) | collective-permute-done | bytes 1048608 | tf_op jit(solution)/shard_map/ppermute | solution.py:73
  488.1 17.2 %collective-permute-done.12 = bf16[128,2048]{1,0:T(8,128)(2,1)S(1)} collective-permute-done((bf16[128,2048]{1,0:T(8,128)(2,1)S(1)}, bf16[128,2048]{1,0:T(8,128)(2,1)S(1)}, u32[]{:S(2)}, u32[]{:S(2)}) %collective-permute-start.12) | collective-permute-done | bytes 524320 | tf_op jit(solution)/shard_map/ppermute | solution.py:62
  564.1 22.4 %collective-permute-done.15 = f32[128,2048]{1,0:T(8,128)} collective-permute-done((f32[128,2048]{1,0:T(8,128)S(1)}, f32[128,2048]{1,0:T(8,128)}, u32[]{:S(2)}, u32[]{:S(2)}) %collective-permute-start.15) | collective-permute-done | bytes 1048608 | tf_op jit(solution)/shard_map/ppermute | solution.py:73
  589.7 7.4 all-to-all-start.1
  601.4 13.9 %copy.92 = bf16[2048,2560]{1,0:T(8,128)(2,1)} copy(bf16[2048,2560]{0,1:T(8,128)(2,1)} %fusion.15) | data formatting | bytes 20971520 | tf_op jit(solution)/shard_map/concatenate | solution.py:209
  615.2 9.8 %all-to-all-start.2 = ((bf16[32,64,2560]{2,1,0:T(8,128)(2,1)}), bf16[32,64,2560]{2,1,0:T(8,128)(2,1)}, u32[]{:S(2)}, u32[]{:S(2)}) async-start(bf16[32,64,2560]{2,1,0:T(8,128)(2,1)} %bitcast.266), calls=%async_computation.2 | async-start | bytes 20971520 | tf_op jit(solution)/shard_map/all_to_all | solution.py:78
  627.0 152.6 %all-to-all-done.2 = bf16[32,64,2560]{2,1,0:T(8,128)(2,1)} async-done(((bf16[32,64,2560]{2,1,0:T(8,128)(2,1)}), bf16[32,64,2560]{2,1,0:T(8,128)(2,1)}, u32[]{:S(2)}, u32[]{:S(2)}) %all-to-all-start.2) | async-done | bytes 10485792 | tf_op jit(solution)/shard_map/all_to_all | solution.py:78
  779.7 5.8 convert_reduce_fusion
  786.3 37.5 %reduce-scatter.4.cloned.1.call-done = bf16[64,4224]{1,0:T(8,128)(2,1)} async-done(((bf16[2048,4224]{1,0:T(8,128)(2,1)}), bf16[64,4224]{1,0:T(8,128)(2,1)}) %reduce-scatter.4.cloned.1.call-update) | async-done | bytes 540688
  (226 shorter events, 167.1 us)
Async XLA Ops:
  7.2 46.2 %copy-start = (s32[1,4,128]{2,1,0:T(4,128)S(1)}, s32[1,4,128]{2,1,0:T(4,128)}, u32[]{:S(2)}) copy-start(s32[1,4,128]{2,1,0:T(4,128)} %param.16) | copy-start | bytes 6148
  7.2 235.8 %all-gather.2.cloned.1.call-start = ((), (), s32[]{:S(2)}) async-start(), calls=%async_computation.4 | async-start | bytes 28655616 | tf_op jit(solution)/shard_map/all_gather | solution.py:130
  16.1 22.1 %all-to-all-start = ((f32[128,3,16]{2,1,0:T(4,128)}), f32[128,3,16]{2,1,0:T(4,128)S(1)}, u32[]{:S(2)}, u32[]{:S(2)}) async-start(f32[128,3,16]{2,1,0:T(4,128)} %broadcast_in_dim.29), calls=%async_computation | async-start | bytes 524288 | tf_op jit(solution)/shard_map/all_to_all | solution.py:85
  27.3 796.6 %reduce-scatter.4.cloned.1.call-start = ((), (), s32[]{:S(2)}) async-start(), calls=%async_computation.5 | async-start | bytes 17842176
  39.0 14.1 %collective-permute-start = (bf16[128,2048]{1,0:T(8,128)(2,1)S(1)}, bf16[128,2048]{1,0:T(8,128)(2,1)S(1)}, u32[]{:S(2)}, u32[]{:S(2)}) collective-permute-start(bf16[128,2048]{1,0:T(8,128)(2,1)S(1)} %fusion.62), channel_id=1, source_target_pairs={{0,2},{2,0},{1,3},{3,1},{4,6},{6,4},{5,7},{7,5},{8,10},{10,8},{9,1... | collective-permute-start | bytes 1572872 | tf_op jit(solution)/shard_map/ppermute | solution.py:62
  53.2 2.9 collective-permute-start.1
  285.2 4.2 collective-permute-start.2
  290.7 37.8 %collective-permute-start.3 = (f32[128,2048]{1,0:T(8,128)}, f32[128,2048]{1,0:T(8,128)}, u32[]{:S(2)}, u32[]{:S(2)}) collective-permute-start(f32[128,2048]{1,0:T(8,128)} %fusion.88), channel_id=1, source_target_pairs={{0,2},{2,0},{1,3},{3,1},{4,6},{6,4},{5,7},{7,5},{8,10},{10,8},{9,1... | collective-permute-start | bytes 3145736 | tf_op jit(solution)/shard_map/ppermute | solution.py:73
  291.6 36.0 %collective-permute-start.8 = (bf16[128,2048]{1,0:T(8,128)(2,1)S(1)}, bf16[128,2048]{1,0:T(8,128)(2,1)S(1)}, u32[]{:S(2)}, u32[]{:S(2)}) collective-permute-start(bf16[128,2048]{1,0:T(8,128)(2,1)S(1)} %bitcast.267), channel_id=1, source_target_pairs={{0,2},{2,0},{1,3},{3,1},{4,6},{6,4},{5,7},{7,5},{8,10},{10,8},{9,1... | collective-permute-start | bytes 1572872 | tf_op jit(solution)/shard_map/ppermute | solution.py:62
  293.2 35.3 %copy-start.14 = (f32[2,128,2048]{2,1,0:T(8,128)S(1)}, f32[2,128,2048]{2,1,0:T(8,128)}, u32[]{:S(2)}) copy-start(f32[2,128,2048]{2,1,0:T(8,128)} %copy-done.13) | copy-start | bytes 6291460
  327.8 16.8 %collective-permute-start.9 = (bf16[2,128,2048]{2,1,0:T(8,128)(2,1)S(1)}, bf16[2,128,2048]{2,1,0:T(8,128)(2,1)S(1)}, u32[]{:S(2)}, u32[]{:S(2)}) collective-permute-start(bf16[2,128,2048]{2,1,0:T(8,128)(2,1)S(1)} %pad_maximum_fusion.7), channel_id=1, source_target_pairs={{0,1},{1,0},{2,3},{3,2},{4,5},{5,4},{6,7},{7,6},{8,9},{9,8},{10,11... | collective-permute-start | bytes 3145736 | tf_op jit(solution)/shard_map/ppermute | solution.py:64
  330.6 13.8 %collective-permute-start.4 = (bf16[128,2048]{1,0:T(8,128)(2,1)S(1)}, bf16[128,2048]{1,0:T(8,128)(2,1)S(1)}, u32[]{:S(2)}, u32[]{:S(2)}) collective-permute-start(bf16[128,2048]{1,0:T(8,128)(2,1)S(1)} %multiply_convert_fusion.4), channel_id=1, source_target_pairs={{0,2},{2,0},{1,3},{3,1},{4,6},{6,4},{5,7},{7,5},{8,10},{10,8},{9,1... | collective-permute-start | bytes 1572872 | tf_op jit(solution)/shard_map/ppermute | solution.py:62
  344.5 6.1 collective-permute-start.5
  415.2 7.7 collective-permute-start.10
  422.1 4.6 collective-permute-start.6
  423.0 33.6 %collective-permute-start.11 = (f32[128,2048]{1,0:T(8,128)S(1)}, f32[128,2048]{1,0:T(8,128)S(1)}, u32[]{:S(2)}, u32[]{:S(2)}) collective-permute-start(f32[128,2048]{1,0:T(8,128)S(1)} %fusion.80), channel_id=1, source_target_pairs={{0,2},{2,0},{1,3},{3,1},{4,6},{6,4},{5,7},{7,5},{8,10},{10,8},{9,1... | collective-permute-start | bytes 3145736 | tf_op jit(solution)/shard_map/ppermute | solution.py:73
  426.8 59.3 %collective-permute-start.7 = (f32[128,2048]{1,0:T(8,128)S(1)}, f32[128,2048]{1,0:T(8,128)S(1)}, u32[]{:S(2)}, u32[]{:S(2)}) collective-permute-start(f32[128,2048]{1,0:T(8,128)S(1)} %fusion.83), channel_id=1, source_target_pairs={{0,2},{2,0},{1,3},{3,1},{4,6},{6,4},{5,7},{7,5},{8,10},{10,8},{9,1... | collective-permute-start | bytes 3145736 | tf_op jit(solution)/shard_map/ppermute | solution.py:73
  487.8 17.5 %collective-permute-start.12 = (bf16[128,2048]{1,0:T(8,128)(2,1)S(1)}, bf16[128,2048]{1,0:T(8,128)(2,1)S(1)}, u32[]{:S(2)}, u32[]{:S(2)}) collective-permute-start(bf16[128,2048]{1,0:T(8,128)(2,1)S(1)} %get-tuple-element.75), channel_id=1, source_target_pairs={{0,2},{2,0},{1,3},{3,1},{4,6},{6,4},{5,7},{7,5},{8,10},{10,8},{9,1... | collective-permute-start | bytes 1572872 | tf_op jit(solution)/shard_map/ppermute | solution.py:62
  505.4 3.0 collective-permute-start.13
  545.9 4.5 collective-permute-start.14
  552.1 34.4 %collective-permute-start.15 = (f32[128,2048]{1,0:T(8,128)S(1)}, f32[128,2048]{1,0:T(8,128)}, u32[]{:S(2)}, u32[]{:S(2)}) collective-permute-start(f32[128,2048]{1,0:T(8,128)S(1)} %fusion.77), channel_id=1, source_target_pairs={{0,2},{2,0},{1,3},{3,1},{4,6},{6,4},{5,7},{7,5},{8,10},{10,8},{9,1... | collective-permute-start | bytes 3145736 | tf_op jit(solution)/shard_map/ppermute | solution.py:73
  564.1 33.0 %copy-start.24 = (bf16[512,512]{1,0:T(8,128)(2,1)S(1)}, bf16[512,512]{1,0:T(8,128)(2,1)}, u32[]{:S(2)}) copy-start(bf16[512,512]{1,0:T(8,128)(2,1)} %copy-done.23) | copy-start | bytes 1572868
  589.7 25.5 %all-to-all-start.1 = ((f32[128,3,16]{2,1,0:T(4,128)}), f32[128,3,16]{2,1,0:T(4,128)S(1)}, u32[]{:S(2)}, u32[]{:S(2)}) async-start(f32[128,3,16]{2,1,0:T(4,128)} %copy.91), calls=%async_computation.1 | async-start | bytes 524288 | tf_op jit(solution)/shard_map/all_to_all | solution.py:92
  615.2 164.4 %all-to-all-start.2 = ((bf16[32,64,2560]{2,1,0:T(8,128)(2,1)}), bf16[32,64,2560]{2,1,0:T(8,128)(2,1)}, u32[]{:S(2)}, u32[]{:S(2)}) async-start(bf16[32,64,2560]{2,1,0:T(8,128)(2,1)} %bitcast.266), calls=%async_computation.2 | async-start | bytes 20971520 | tf_op jit(solution)/shard_map/all_to_all | solution.py:78
  (40 other events, 286.0 us)
Sparse Core Ops, SparseCore 0:
  15.4 227.5 all-gather.1
  403.5 420.2 reduce-scatter.3
